TPU v7x, 512 devices: a whole 4x8x8 slice. The times are simulated.
512 devices in a mesh: blk: 64 (over y, x, z_lo), rep: 8 (over z_hi, core).
Axes of the slice: x: 4, y: 8, z: 8 (z_hi: 4, z_lo: 2; z = z_hi * 2 + z_lo), core: 2. Of those that a mesh axis runs over, the one named last changes fastest.
Arguments:
- features: bfloat16 [65536, 256], P(('blk', 'rep')), may hold values from -6 to 6
- degrees: int32 [65536], P(('blk', 'rep')), may hold values from 4 to 64
- tile_values: bfloat16 [512, 16, 8, 128, 128], P(('blk', 'rep')), may hold values from 0 to 1
- tile_rows: int32 [512, 16, 8], P(('blk', 'rep')), may hold values from 0 to 7, as said below
- tile_counts: int32 [512, 16], P(('blk', 'rep')), may hold values from 1 to 8, as said below
- weight: bfloat16 [256, 256], replicated, may hold values from -0.375 to 0.375
- cotangent: bfloat16 [65536, 256], P(('blk', 'rep')), may hold values from -6 to 6
Outputs:
- activations: bfloat16 [65536, 256], P(('blk', 'rep'))
- grad_weight: float32 [256, 256], replicated
- grad_features: bfloat16 [65536, 256], P(('blk', 'rep'))
Inputs may be any that keep to these rules, and one draw needn't show every extreme that they name: `tile_rows`: the 8 slots of one owner and distance name the 8 row blocks of its slab, each once. Only the first tile_counts[o, s] slots of owner o and distance s are live. In every draw some slab has all 8 slots live at every distance for every owner in it.
All inputs are finite; a program needn't handle non-finite values.
Results may differ from a plain program's by a relative error of at most 0.0077.
Values may be sent and summed in bfloat16 or wider, within the bound.
No kernel may reach another device: no remote copies, remote signals or barrier semaphores. Data moves between devices by JAX's collectives and lax.ppermute only.
A program may use at most 64 MiB of HBM per device.

v0:
```python
import math
import jax
import jax.numpy as jnp
from jax import lax
from jax.sharding import PartitionSpec as P


def passed_along(block, axis, distance):
    devices = range(lax.axis_size(axis))
    route = [((i - distance) % len(devices), i) for i in devices]
    return lax.ppermute(block, axis, route)


def per_device(features, degrees, tile_values, tile_rows, tile_counts, weight, cotangent):
    own_rows = features.shape[0]
    feature_width = features.shape[1]
    span_count = tile_values.shape[1]
    slot_count = tile_values.shape[2]
    block_size = tile_values.shape[3]
    inv_root = lax.rsqrt(degrees.astype(jnp.float32))[:, None]
    scaled = (features.astype(jnp.float32) * inv_root).astype(jnp.bfloat16)
    tile_stack = tile_values[0]
    row_stack = tile_rows[0]
    count_stack = tile_counts[0]
    slot_ids = jnp.arange(slot_count, dtype=jnp.int32)

    def load_distance(distance):
        tile_block = lax.dynamic_index_in_dim(tile_stack, distance, 0, keepdims=False)
        row_ids = lax.dynamic_index_in_dim(row_stack, distance, 0, keepdims=False)
        live_count = lax.dynamic_index_in_dim(count_stack, distance, 0, keepdims=False)
        return (tile_block, row_ids, live_count)

    def gather_rows(partial_sum, distance, source_rows):
        tile_block, row_ids, live_count = load_distance(distance)
        match_table = row_ids[None, :] == slot_ids[:, None]
        slot_of_row = jnp.sum(jnp.where(match_table, slot_ids[None, :], 0), axis=1)
        arranged = jnp.take(tile_block, slot_of_row, axis=0)
        row_live = slot_of_row < live_count
        product = jnp.einsum(
            "mij,jf->mif", arranged, source_rows, preferred_element_type=jnp.float32
        )
        return partial_sum + jnp.where(row_live[:, None, None], product, 0.0)

    def forward_turn(distance, carry):
        partial_sum, source_rows = carry
        partial_sum = gather_rows(partial_sum, distance, source_rows)
        source_rows = passed_along(source_rows, "blk", 1)
        return (partial_sum, source_rows)

    start_total = jnp.zeros((slot_count, block_size, feature_width), jnp.float32)
    partial_sum, source_rows = lax.fori_loop(0, span_count - 1, forward_turn, (start_total, scaled))
    partial_sum = gather_rows(partial_sum, span_count - 1, source_rows)
    slab_partial = partial_sum.reshape(slot_count * block_size, feature_width)
    own_sum = lax.psum_scatter(slab_partial, "rep", scatter_dimension=0, tiled=True)
    aggregated = (own_sum * inv_root).astype(jnp.bfloat16)
    pre_act = jnp.dot(aggregated, weight, preferred_element_type=jnp.float32)
    sigma = jax.nn.sigmoid(pre_act)
    activations = (pre_act * sigma).astype(jnp.bfloat16)
    act_grad = (cotangent.astype(jnp.float32) * sigma * (1.0 + pre_act * (1.0 - sigma))).astype(
        jnp.bfloat16
    )
    local_weight = lax.dot_general(
        aggregated, act_grad, (((0,), (0,)), ((), ())), preferred_element_type=jnp.float32
    )
    node_total = own_rows * lax.axis_size("blk") * lax.axis_size("rep")
    grad_weight = lax.psum(local_weight, ("blk", "rep")) / math.sqrt(node_total)
    back_grad = lax.dot_general(
        act_grad, weight, (((1,), (1,)), ((), ())), preferred_element_type=jnp.float32
    )
    back_scaled = (back_grad * inv_root).astype(jnp.bfloat16)
    slab_grads = lax.all_gather(back_scaled, "rep", axis=0, tiled=True).reshape(
        slot_count, block_size, feature_width
    )

    def scatter_rows(back_sum, distance):
        tile_block, row_ids, live_count = load_distance(distance)
        picked = jnp.take(slab_grads, row_ids, axis=0)
        picked = jnp.where((slot_ids < live_count)[:, None, None], picked, jnp.zeros_like(picked))
        return back_sum + jnp.einsum(
            "kij,kif->jf", tile_block, picked, preferred_element_type=jnp.float32
        )

    def backward_turn(turn_index, back_sum):
        back_sum = scatter_rows(back_sum, span_count - 1 - turn_index)
        return passed_along(back_sum, "blk", -1)

    zero_back = jnp.zeros((own_rows, feature_width), jnp.float32)
    back_total = lax.fori_loop(0, span_count - 1, backward_turn, zero_back)
    back_total = scatter_rows(back_total, 0)
    grad_features = (back_total * inv_root).astype(jnp.bfloat16)
    return (activations, grad_weight, grad_features)


def solution(mesh):
    placed = (
        P(("blk", "rep"), None),
        P(("blk", "rep")),
        P(("blk", "rep"), None, None, None, None),
        P(("blk", "rep"), None, None),
        P(("blk", "rep"), None),
        P(),
        P(("blk", "rep"), None),
    )
    return jax.shard_map(
        per_device,
        mesh=mesh,
        in_specs=placed,
        out_specs=(P(("blk", "rep"), None), P(), P(("blk", "rep"), None)),
        check_vma=False,
    )
```

profile of v0, /device:TPU:23, one launch (start us, length us, event | category | flops | bytes accessed | tf_op | source)
XLA Modules:
  0.0 516.1 jit_solution(8821793906793815661)
XLA Ops:
  14.3 121.5 %while.34 = (s32[]{:T(128)}, f32[8,128,256]{2,1,0:T(8,128)S(1)}, bf16[128,256]{1,0:T(8,128)(2,1)S(1)}, s32[16,8]{1,0:T(8,128)S(1)}, s32[16]{0:T(128)}, /*index=5...) while((s32[]{:T(128)}, f32[8,128,256]{2,1,0:T(8,128)S(1)}, ...), condition=%wide.region_2.4_spmd.clone.clone, body=%wide.region_0.3_spmd.clone.clone.sunk | while | flops 68027656 | bytes 3871199 | solution.py:51
  14.3 4.0 collective-permute-start.1
  29.2 4.0 collective-permute-start.1
  37.5 3.7 collective-permute-start.1
  53.6 3.7 collective-permute-start.1
  61.6 3.7 collective-permute-start.1
  69.6 3.7 collective-permute-start.1
  85.6 4.1 collective-permute-start.1
  94.0 3.7 collective-permute-start.1
  102.0 3.7 collective-permute-start.1
  110.0 3.7 collective-permute-start.1
  118.1 4.2 collective-permute-start.1
  126.6 4.9 collective-permute-start.1
  137.9 77.7 %reduce-scatter.2.cloned.1.call-done = f32[128,256]{1,0:T(8,128)} async-done(((f32[1024,256]{1,0:T(8,128)}), f32[128,256]{1,0:T(8,128)}) %reduce-scatter.2.cloned.1.call-update) | async-done | bytes 131088 | tf_op jit(solution)/shard_map/reduce_scatter | solution.py:54
  217.6 17.1 %all_gather.3 = bf16[1024,256]{1,0:T(8,128)(2,1)S(1)} all-gather(bf16[128,256]{1,0:T(8,128)(2,1)S(1)} %fusion.25), channel_id=1, replica_groups=mesh['blk'=64,'rep'=8] {'rep'}, dimensions={0}, use_global_device_ids=true | all-gather | bytes 589824 | tf_op jit(solution)/shard_map/all_gather | solution.py:71
  237.3 179.3 %while.33 = (s32[]{:T(128)}, f32[128,256]{1,0:T(8,128)S(1)}, bf16[16,8,128,128]{3,2,1,0:T(8,128)(2,1)}, s32[16]{0:T(128)S(1)}, s32[16,8]{1,0:T(8,128)S(1)}, /*in...) while((s32[]{:T(128)}, f32[128,256]{1,0:T(8,128)S(1)}, ...), condition=%wide.region_7.10_spmd.clone, body=%wide.region_6.9_spmd.clone.sunk | while | flops 67667008 | bytes 2625907 | solution.py:88
  242.7 4.7 collective-permute-done
  253.6 4.8 collective-permute-done
  263.6 6.5 %collective-permute-done = f32[128,256]{1,0:T(8,128)S(1)} collective-permute-done((f32[128,256]{1,0:T(8,128)S(1)}, f32[128,256]{1,0:T(8,128)S(1)}, u32[]{:S(2)}, u32[]{:S(2)}) %collective-permute-start) | collective-permute-done | bytes 131104 | tf_op jit(solution)/shard_map/while/body/eval_jaxpr/ppermute | solution.py:11
  275.3 6.8 %collective-permute-done = f32[128,256]{1,0:T(8,128)S(1)} collective-permute-done((f32[128,256]{1,0:T(8,128)S(1)}, f32[128,256]{1,0:T(8,128)S(1)}, u32[]{:S(2)}, u32[]{:S(2)}) %collective-permute-start) | collective-permute-done | bytes 131104 | tf_op jit(solution)/shard_map/while/body/eval_jaxpr/ppermute | solution.py:11
  287.2 6.7 %collective-permute-done = f32[128,256]{1,0:T(8,128)S(1)} collective-permute-done((f32[128,256]{1,0:T(8,128)S(1)}, f32[128,256]{1,0:T(8,128)S(1)}, u32[]{:S(2)}, u32[]{:S(2)}) %collective-permute-start) | collective-permute-done | bytes 131104 | tf_op jit(solution)/shard_map/while/body/eval_jaxpr/ppermute | solution.py:11
  299.1 6.7 %collective-permute-done = f32[128,256]{1,0:T(8,128)S(1)} collective-permute-done((f32[128,256]{1,0:T(8,128)S(1)}, f32[128,256]{1,0:T(8,128)S(1)}, u32[]{:S(2)}, u32[]{:S(2)}) %collective-permute-start) | collective-permute-done | bytes 131104 | tf_op jit(solution)/shard_map/while/body/eval_jaxpr/ppermute | solution.py:11
  311.0 7.2 %collective-permute-done = f32[128,256]{1,0:T(8,128)S(1)} collective-permute-done((f32[128,256]{1,0:T(8,128)S(1)}, f32[128,256]{1,0:T(8,128)S(1)}, u32[]{:S(2)}, u32[]{:S(2)}) %collective-permute-start) | collective-permute-done | bytes 131104 | tf_op jit(solution)/shard_map/while/body/eval_jaxpr/ppermute | solution.py:11
  323.4 6.9 %collective-permute-done = f32[128,256]{1,0:T(8,128)S(1)} collective-permute-done((f32[128,256]{1,0:T(8,128)S(1)}, f32[128,256]{1,0:T(8,128)S(1)}, u32[]{:S(2)}, u32[]{:S(2)}) %collective-permute-start) | collective-permute-done | bytes 131104 | tf_op jit(solution)/shard_map/while/body/eval_jaxpr/ppermute | solution.py:11
  335.5 6.3 %collective-permute-done = f32[128,256]{1,0:T(8,128)S(1)} collective-permute-done((f32[128,256]{1,0:T(8,128)S(1)}, f32[128,256]{1,0:T(8,128)S(1)}, u32[]{:S(2)}, u32[]{:S(2)}) %collective-permute-start) | collective-permute-done | bytes 131104 | tf_op jit(solution)/shard_map/while/body/eval_jaxpr/ppermute | solution.py:11
  347.1 7.2 %collective-permute-done = f32[128,256]{1,0:T(8,128)S(1)} collective-permute-done((f32[128,256]{1,0:T(8,128)S(1)}, f32[128,256]{1,0:T(8,128)S(1)}, u32[]{:S(2)}, u32[]{:S(2)}) %collective-permute-start) | collective-permute-done | bytes 131104 | tf_op jit(solution)/shard_map/while/body/eval_jaxpr/ppermute | solution.py:11
  359.5 6.6 %collective-permute-done = f32[128,256]{1,0:T(8,128)S(1)} collective-permute-done((f32[128,256]{1,0:T(8,128)S(1)}, f32[128,256]{1,0:T(8,128)S(1)}, u32[]{:S(2)}, u32[]{:S(2)}) %collective-permute-start) | collective-permute-done | bytes 131104 | tf_op jit(solution)/shard_map/while/body/eval_jaxpr/ppermute | solution.py:11
  371.3 8.0 %collective-permute-done = f32[128,256]{1,0:T(8,128)S(1)} collective-permute-done((f32[128,256]{1,0:T(8,128)S(1)}, f32[128,256]{1,0:T(8,128)S(1)}, u32[]{:S(2)}, u32[]{:S(2)}) %collective-permute-start) | collective-permute-done | bytes 131104 | tf_op jit(solution)/shard_map/while/body/eval_jaxpr/ppermute | solution.py:11
  384.4 8.5 %collective-permute-done = f32[128,256]{1,0:T(8,128)S(1)} collective-permute-done((f32[128,256]{1,0:T(8,128)S(1)}, f32[128,256]{1,0:T(8,128)S(1)}, u32[]{:S(2)}, u32[]{:S(2)}) %collective-permute-start) | collective-permute-done | bytes 131104 | tf_op jit(solution)/shard_map/while/body/eval_jaxpr/ppermute | solution.py:11
  398.2 6.4 %collective-permute-done = f32[128,256]{1,0:T(8,128)S(1)} collective-permute-done((f32[128,256]{1,0:T(8,128)S(1)}, f32[128,256]{1,0:T(8,128)S(1)}, u32[]{:S(2)}, u32[]{:S(2)}) %collective-permute-start) | collective-permute-done | bytes 131104 | tf_op jit(solution)/shard_map/while/body/eval_jaxpr/ppermute | solution.py:11
  409.8 6.8 %collective-permute-done = f32[128,256]{1,0:T(8,128)S(1)} collective-permute-done((f32[128,256]{1,0:T(8,128)S(1)}, f32[128,256]{1,0:T(8,128)S(1)}, u32[]{:S(2)}, u32[]{:S(2)}) %collective-permute-start) | collective-permute-done | bytes 131104 | tf_op jit(solution)/shard_map/while/body/eval_jaxpr/ppermute | solution.py:11
  418.5 89.1 %all-reduce.2.cloned.1.call-done = f32[256,256]{1,0:T(8,128)} async-done(((f32[256,256]{1,0:T(8,128)}), f32[256,256]{1,0:T(8,128)}) %all-reduce.2.cloned.1.call-update) | async-done | bytes 262160 | tf_op jit(solution)/shard_map/psum | solution.py:66
  (291 shorter events, 169.1 us)
Async XLA Ops:
  7.2 208.4 %reduce-scatter.2.cloned.1.call-start = ((), (), s32[]{:S(2)}) async-start(), calls=%async_computation.1 | async-start | bytes 1179648 | tf_op jit(solution)/shard_map/reduce_scatter | solution.py:54
  14.3 8.3 %collective-permute-start.1 = (bf16[128,256]{1,0:T(8,128)(2,1)S(1)}, bf16[128,256]{1,0:T(8,128)(2,1)S(1)}, u32[]{:S(2)}, u32[]{:S(2)}) collective-permute-start(bf16[128,256]{1,0:T(8,128)(2,1)S(1)} %copy.29), channel_id=1, source_target_pairs={{504,0},{0,8},{8,16},{16,24},{24,32},{32,40},{40,48},{48,56},{56,6... | collective-permute-start | bytes 196616 | tf_op jit(solution)/shard_map/while/body/eval_jaxpr/ppermute | solution.py:11
  22.6 6.5 %collective-permute-start.1 = (bf16[128,256]{1,0:T(8,128)(2,1)S(1)}, bf16[128,256]{1,0:T(8,128)(2,1)S(1)}, u32[]{:S(2)}, u32[]{:S(2)}) collective-permute-start(bf16[128,256]{1,0:T(8,128)(2,1)S(1)} %copy.29), channel_id=1, source_target_pairs={{504,0},{0,8},{8,16},{16,24},{24,32},{32,40},{40,48},{48,56},{56,6... | collective-permute-start | bytes 196616 | tf_op jit(solution)/shard_map/while/body/eval_jaxpr/ppermute | solution.py:11
  29.2 8.3 %collective-permute-start.1 = (bf16[128,256]{1,0:T(8,128)(2,1)S(1)}, bf16[128,256]{1,0:T(8,128)(2,1)S(1)}, u32[]{:S(2)}, u32[]{:S(2)}) collective-permute-start(bf16[128,256]{1,0:T(8,128)(2,1)S(1)} %copy.29), channel_id=1, source_target_pairs={{504,0},{0,8},{8,16},{16,24},{24,32},{32,40},{40,48},{48,56},{56,6... | collective-permute-start | bytes 196616 | tf_op jit(solution)/shard_map/while/body/eval_jaxpr/ppermute | solution.py:11
  37.5 8.0 %collective-permute-start.1 = (bf16[128,256]{1,0:T(8,128)(2,1)S(1)}, bf16[128,256]{1,0:T(8,128)(2,1)S(1)}, u32[]{:S(2)}, u32[]{:S(2)}) collective-permute-start(bf16[128,256]{1,0:T(8,128)(2,1)S(1)} %copy.29), channel_id=1, source_target_pairs={{504,0},{0,8},{8,16},{16,24},{24,32},{32,40},{40,48},{48,56},{56,6... | collective-permute-start | bytes 196616 | tf_op jit(solution)/shard_map/while/body/eval_jaxpr/ppermute | solution.py:11
  45.6 8.0 %collective-permute-start.1 = (bf16[128,256]{1,0:T(8,128)(2,1)S(1)}, bf16[128,256]{1,0:T(8,128)(2,1)S(1)}, u32[]{:S(2)}, u32[]{:S(2)}) collective-permute-start(bf16[128,256]{1,0:T(8,128)(2,1)S(1)} %copy.29), channel_id=1, source_target_pairs={{504,0},{0,8},{8,16},{16,24},{24,32},{32,40},{40,48},{48,56},{56,6... | collective-permute-start | bytes 196616 | tf_op jit(solution)/shard_map/while/body/eval_jaxpr/ppermute | solution.py:11
  53.6 8.0 %collective-permute-start.1 = (bf16[128,256]{1,0:T(8,128)(2,1)S(1)}, bf16[128,256]{1,0:T(8,128)(2,1)S(1)}, u32[]{:S(2)}, u32[]{:S(2)}) collective-permute-start(bf16[128,256]{1,0:T(8,128)(2,1)S(1)} %copy.29), channel_id=1, source_target_pairs={{504,0},{0,8},{8,16},{16,24},{24,32},{32,40},{40,48},{48,56},{56,6... | collective-permute-start | bytes 196616 | tf_op jit(solution)/shard_map/while/body/eval_jaxpr/ppermute | solution.py:11
  61.6 8.0 %collective-permute-start.1 = (bf16[128,256]{1,0:T(8,128)(2,1)S(1)}, bf16[128,256]{1,0:T(8,128)(2,1)S(1)}, u32[]{:S(2)}, u32[]{:S(2)}) collective-permute-start(bf16[128,256]{1,0:T(8,128)(2,1)S(1)} %copy.29), channel_id=1, source_target_pairs={{504,0},{0,8},{8,16},{16,24},{24,32},{32,40},{40,48},{48,56},{56,6... | collective-permute-start | bytes 196616 | tf_op jit(solution)/shard_map/while/body/eval_jaxpr/ppermute | solution.py:11
  69.6 8.0 %collective-permute-start.1 = (bf16[128,256]{1,0:T(8,128)(2,1)S(1)}, bf16[128,256]{1,0:T(8,128)(2,1)S(1)}, u32[]{:S(2)}, u32[]{:S(2)}) collective-permute-start(bf16[128,256]{1,0:T(8,128)(2,1)S(1)} %copy.29), channel_id=1, source_target_pairs={{504,0},{0,8},{8,16},{16,24},{24,32},{32,40},{40,48},{48,56},{56,6... | collective-permute-start | bytes 196616 | tf_op jit(solution)/shard_map/while/body/eval_jaxpr/ppermute | solution.py:11
  77.6 8.0 %collective-permute-start.1 = (bf16[128,256]{1,0:T(8,128)(2,1)S(1)}, bf16[128,256]{1,0:T(8,128)(2,1)S(1)}, u32[]{:S(2)}, u32[]{:S(2)}) collective-permute-start(bf16[128,256]{1,0:T(8,128)(2,1)S(1)} %copy.29), channel_id=1, source_target_pairs={{504,0},{0,8},{8,16},{16,24},{24,32},{32,40},{40,48},{48,56},{56,6... | collective-permute-start | bytes 196616 | tf_op jit(solution)/shard_map/while/body/eval_jaxpr/ppermute | solution.py:11
  85.6 8.4 %collective-permute-start.1 = (bf16[128,256]{1,0:T(8,128)(2,1)S(1)}, bf16[128,256]{1,0:T(8,128)(2,1)S(1)}, u32[]{:S(2)}, u32[]{:S(2)}) collective-permute-start(bf16[128,256]{1,0:T(8,128)(2,1)S(1)} %copy.29), channel_id=1, source_target_pairs={{504,0},{0,8},{8,16},{16,24},{24,32},{32,40},{40,48},{48,56},{56,6... | collective-permute-start | bytes 196616 | tf_op jit(solution)/shard_map/while/body/eval_jaxpr/ppermute | solution.py:11
  94.0 8.0 %collective-permute-start.1 = (bf16[128,256]{1,0:T(8,128)(2,1)S(1)}, bf16[128,256]{1,0:T(8,128)(2,1)S(1)}, u32[]{:S(2)}, u32[]{:S(2)}) collective-permute-start(bf16[128,256]{1,0:T(8,128)(2,1)S(1)} %copy.29), channel_id=1, source_target_pairs={{504,0},{0,8},{8,16},{16,24},{24,32},{32,40},{40,48},{48,56},{56,6... | collective-permute-start | bytes 196616 | tf_op jit(solution)/shard_map/while/body/eval_jaxpr/ppermute | solution.py:11
  102.0 8.0 %collective-permute-start.1 = (bf16[128,256]{1,0:T(8,128)(2,1)S(1)}, bf16[128,256]{1,0:T(8,128)(2,1)S(1)}, u32[]{:S(2)}, u32[]{:S(2)}) collective-permute-start(bf16[128,256]{1,0:T(8,128)(2,1)S(1)} %copy.29), channel_id=1, source_target_pairs={{504,0},{0,8},{8,16},{16,24},{24,32},{32,40},{40,48},{48,56},{56,6... | collective-permute-start | bytes 196616 | tf_op jit(solution)/shard_map/while/body/eval_jaxpr/ppermute | solution.py:11
  110.0 8.0 %collective-permute-start.1 = (bf16[128,256]{1,0:T(8,128)(2,1)S(1)}, bf16[128,256]{1,0:T(8,128)(2,1)S(1)}, u32[]{:S(2)}, u32[]{:S(2)}) collective-permute-start(bf16[128,256]{1,0:T(8,128)(2,1)S(1)} %copy.29), channel_id=1, source_target_pairs={{504,0},{0,8},{8,16},{16,24},{24,32},{32,40},{40,48},{48,56},{56,6... | collective-permute-start | bytes 196616 | tf_op jit(solution)/shard_map/while/body/eval_jaxpr/ppermute | solution.py:11
  118.1 8.5 %collective-permute-start.1 = (bf16[128,256]{1,0:T(8,128)(2,1)S(1)}, bf16[128,256]{1,0:T(8,128)(2,1)S(1)}, u32[]{:S(2)}, u32[]{:S(2)}) collective-permute-start(bf16[128,256]{1,0:T(8,128)(2,1)S(1)} %copy.29), channel_id=1, source_target_pairs={{504,0},{0,8},{8,16},{16,24},{24,32},{32,40},{40,48},{48,56},{56,6... | collective-permute-start | bytes 196616 | tf_op jit(solution)/shard_map/while/body/eval_jaxpr/ppermute | solution.py:11
  126.6 9.2 %collective-permute-start.1 = (bf16[128,256]{1,0:T(8,128)(2,1)S(1)}, bf16[128,256]{1,0:T(8,128)(2,1)S(1)}, u32[]{:S(2)}, u32[]{:S(2)}) collective-permute-start(bf16[128,256]{1,0:T(8,128)(2,1)S(1)} %copy.29), channel_id=1, source_target_pairs={{504,0},{0,8},{8,16},{16,24},{24,32},{32,40},{40,48},{48,56},{56,6... | collective-permute-start | bytes 196616 | tf_op jit(solution)/shard_map/while/body/eval_jaxpr/ppermute | solution.py:11
  137.2 370.4 %all-reduce.2.cloned.1.call-start = ((), (), s32[]{:S(2)}) async-start(), calls=%async_computation.2 | async-start | bytes 524288 | tf_op jit(solution)/shard_map/psum | solution.py:66
  240.6 6.8 %collective-permute-start = (f32[128,256]{1,0:T(8,128)S(1)}, f32[128,256]{1,0:T(8,128)S(1)}, u32[]{:S(2)}, u32[]{:S(2)}) collective-permute-start(f32[128,256]{1,0:T(8,128)S(1)} %fusion.53), channel_id=1, source_target_pairs={{8,0},{16,8},{24,16},{32,24},{40,32},{48,40},{56,48},{64,56},{72,6... | collective-permute-start | bytes 393224 | tf_op jit(solution)/shard_map/while/body/eval_jaxpr/ppermute | solution.py:11
  250.6 7.8 %collective-permute-start = (f32[128,256]{1,0:T(8,128)S(1)}, f32[128,256]{1,0:T(8,128)S(1)}, u32[]{:S(2)}, u32[]{:S(2)}) collective-permute-start(f32[128,256]{1,0:T(8,128)S(1)} %fusion.53), channel_id=1, source_target_pairs={{8,0},{16,8},{24,16},{32,24},{40,32},{48,40},{56,48},{64,56},{72,6... | collective-permute-start | bytes 393224 | tf_op jit(solution)/shard_map/while/body/eval_jaxpr/ppermute | solution.py:11
  261.6 8.4 %collective-permute-start = (f32[128,256]{1,0:T(8,128)S(1)}, f32[128,256]{1,0:T(8,128)S(1)}, u32[]{:S(2)}, u32[]{:S(2)}) collective-permute-start(f32[128,256]{1,0:T(8,128)S(1)} %fusion.53), channel_id=1, source_target_pairs={{8,0},{16,8},{24,16},{32,24},{40,32},{48,40},{56,48},{64,56},{72,6... | collective-permute-start | bytes 393224 | tf_op jit(solution)/shard_map/while/body/eval_jaxpr/ppermute | solution.py:11
  273.3 8.7 %collective-permute-start = (f32[128,256]{1,0:T(8,128)S(1)}, f32[128,256]{1,0:T(8,128)S(1)}, u32[]{:S(2)}, u32[]{:S(2)}) collective-permute-start(f32[128,256]{1,0:T(8,128)S(1)} %fusion.53), channel_id=1, source_target_pairs={{8,0},{16,8},{24,16},{32,24},{40,32},{48,40},{56,48},{64,56},{72,6... | collective-permute-start | bytes 393224 | tf_op jit(solution)/shard_map/while/body/eval_jaxpr/ppermute | solution.py:11
  285.3 8.6 %collective-permute-start = (f32[128,256]{1,0:T(8,128)S(1)}, f32[128,256]{1,0:T(8,128)S(1)}, u32[]{:S(2)}, u32[]{:S(2)}) collective-permute-start(f32[128,256]{1,0:T(8,128)S(1)} %fusion.53), channel_id=1, source_target_pairs={{8,0},{16,8},{24,16},{32,24},{40,32},{48,40},{56,48},{64,56},{72,6... | collective-permute-start | bytes 393224 | tf_op jit(solution)/shard_map/while/body/eval_jaxpr/ppermute | solution.py:11
  297.2 8.6 %collective-permute-start = (f32[128,256]{1,0:T(8,128)S(1)}, f32[128,256]{1,0:T(8,128)S(1)}, u32[]{:S(2)}, u32[]{:S(2)}) collective-permute-start(f32[128,256]{1,0:T(8,128)S(1)} %fusion.53), channel_id=1, source_target_pairs={{8,0},{16,8},{24,16},{32,24},{40,32},{48,40},{56,48},{64,56},{72,6... | collective-permute-start | bytes 393224 | tf_op jit(solution)/shard_map/while/body/eval_jaxpr/ppermute | solution.py:11
  309.1 9.1 %collective-permute-start = (f32[128,256]{1,0:T(8,128)S(1)}, f32[128,256]{1,0:T(8,128)S(1)}, u32[]{:S(2)}, u32[]{:S(2)}) collective-permute-start(f32[128,256]{1,0:T(8,128)S(1)} %fusion.53), channel_id=1, source_target_pairs={{8,0},{16,8},{24,16},{32,24},{40,32},{48,40},{56,48},{64,56},{72,6... | collective-permute-start | bytes 393224 | tf_op jit(solution)/shard_map/while/body/eval_jaxpr/ppermute | solution.py:11
  321.5 8.9 %collective-permute-start = (f32[128,256]{1,0:T(8,128)S(1)}, f32[128,256]{1,0:T(8,128)S(1)}, u32[]{:S(2)}, u32[]{:S(2)}) collective-permute-start(f32[128,256]{1,0:T(8,128)S(1)} %fusion.53), channel_id=1, source_target_pairs={{8,0},{16,8},{24,16},{32,24},{40,32},{48,40},{56,48},{64,56},{72,6... | collective-permute-start | bytes 393224 | tf_op jit(solution)/shard_map/while/body/eval_jaxpr/ppermute | solution.py:11
  333.6 8.3 %collective-permute-start = (f32[128,256]{1,0:T(8,128)S(1)}, f32[128,256]{1,0:T(8,128)S(1)}, u32[]{:S(2)}, u32[]{:S(2)}) collective-permute-start(f32[128,256]{1,0:T(8,128)S(1)} %fusion.53), channel_id=1, source_target_pairs={{8,0},{16,8},{24,16},{32,24},{40,32},{48,40},{56,48},{64,56},{72,6... | collective-permute-start | bytes 393224 | tf_op jit(solution)/shard_map/while/body/eval_jaxpr/ppermute | solution.py:11
  345.1 9.2 %collective-permute-start = (f32[128,256]{1,0:T(8,128)S(1)}, f32[128,256]{1,0:T(8,128)S(1)}, u32[]{:S(2)}, u32[]{:S(2)}) collective-permute-start(f32[128,256]{1,0:T(8,128)S(1)} %fusion.53), channel_id=1, source_target_pairs={{8,0},{16,8},{24,16},{32,24},{40,32},{48,40},{56,48},{64,56},{72,6... | collective-permute-start | bytes 393224 | tf_op jit(solution)/shard_map/while/body/eval_jaxpr/ppermute | solution.py:11
  357.5 8.5 %collective-permute-start = (f32[128,256]{1,0:T(8,128)S(1)}, f32[128,256]{1,0:T(8,128)S(1)}, u32[]{:S(2)}, u32[]{:S(2)}) collective-permute-start(f32[128,256]{1,0:T(8,128)S(1)} %fusion.53), channel_id=1, source_target_pairs={{8,0},{16,8},{24,16},{32,24},{40,32},{48,40},{56,48},{64,56},{72,6... | collective-permute-start | bytes 393224 | tf_op jit(solution)/shard_map/while/body/eval_jaxpr/ppermute | solution.py:11
  369.3 9.9 %collective-permute-start = (f32[128,256]{1,0:T(8,128)S(1)}, f32[128,256]{1,0:T(8,128)S(1)}, u32[]{:S(2)}, u32[]{:S(2)}) collective-permute-start(f32[128,256]{1,0:T(8,128)S(1)} %fusion.53), channel_id=1, source_target_pairs={{8,0},{16,8},{24,16},{32,24},{40,32},{48,40},{56,48},{64,56},{72,6... | collective-permute-start | bytes 393224 | tf_op jit(solution)/shard_map/while/body/eval_jaxpr/ppermute | solution.py:11
  382.5 10.5 %collective-permute-start = (f32[128,256]{1,0:T(8,128)S(1)}, f32[128,256]{1,0:T(8,128)S(1)}, u32[]{:S(2)}, u32[]{:S(2)}) collective-permute-start(f32[128,256]{1,0:T(8,128)S(1)} %fusion.53), channel_id=1, source_target_pairs={{8,0},{16,8},{24,16},{32,24},{40,32},{48,40},{56,48},{64,56},{72,6... | collective-permute-start | bytes 393224 | tf_op jit(solution)/shard_map/while/body/eval_jaxpr/ppermute | solution.py:11
  396.2 8.3 %collective-permute-start = (f32[128,256]{1,0:T(8,128)S(1)}, f32[128,256]{1,0:T(8,128)S(1)}, u32[]{:S(2)}, u32[]{:S(2)}) collective-permute-start(f32[128,256]{1,0:T(8,128)S(1)} %fusion.53), channel_id=1, source_target_pairs={{8,0},{16,8},{24,16},{32,24},{40,32},{48,40},{56,48},{64,56},{72,6... | collective-permute-start | bytes 393224 | tf_op jit(solution)/shard_map/while/body/eval_jaxpr/ppermute | solution.py:11
  407.8 8.7 %collective-permute-start = (f32[128,256]{1,0:T(8,128)S(1)}, f32[128,256]{1,0:T(8,128)S(1)}, u32[]{:S(2)}, u32[]{:S(2)}) collective-permute-start(f32[128,256]{1,0:T(8,128)S(1)} %fusion.53), channel_id=1, source_target_pairs={{8,0},{16,8},{24,16},{32,24},{40,32},{48,40},{56,48},{64,56},{72,6... | collective-permute-start | bytes 393224 | tf_op jit(solution)/shard_map/while/body/eval_jaxpr/ppermute | solution.py:11
  (3 other events, 511.3 us)
Sparse Core Ops, SparseCore 0:
  137.3 78.3 reduce-scatter.1
  236.8 270.7 all-reduce.1
where the time goes:
time: 519 us; the launch traced here: 516 us
  waiting for transfers between devices  267 us (51%)
  starting transfers between devices  86.5 us (17%)
  local copies, waits for them, and re-layouts  66.3 us (13%)
  matrix products  36.1 us (7%)
  other arithmetic  26.9 us (5%)
  blocking collectives  17.1 us (3%)
  between operations  14.2 us (3%)
    ppermute x30, waiting for transfers between devices, passed_along(): return lax.ppermute(block, axis, route)  100 us
    psum x1, waiting for transfers between devices, per_device(): grad_weight = lax.psum(local_weight, ('blk', 'rep')) / math.sqrt(node_total)  89.1 us
    ppermute x30, starting transfers between devices, passed_along(): return lax.ppermute(block, axis, route)  86.4 us
    reduce_scatter x1, waiting for transfers between devices, per_device(): lax.psum_scatter(slab_partial, 'rep', scatter_dimension=0, tiled=True)  77.7 us
    dynamic_slice x31, local copies, waits for them, and re-layouts, load_distance(): lax.dynamic_index_in_dim(count_stack, distance, 0, keepdims=False)  29.8 us
    dot_general x16, matrix products, scatter_rows(): jnp.einsum('kij,kif->jf', tile_block, picked, preferred_element_type=jnp....  21.2 us
    all_gather x1, blocking collectives, per_device(): lax.all_gather(back_scaled, 'rep', axis=0, tiled=True)  17.1 us
    squeeze x16, local copies, waits for them, and re-layouts, load_distance(): lax.dynamic_index_in_dim(tile_stack, distance, 0, keepdims=False)  15.6 us
  transfers between devices with their start and end apart: 32, of which 17 were waited for; matrix products, arithmetic and copies ran while one was open for 22% of the time, Pallas kernels for 0%

commit v1 on v0

--- a/solution.py
+++ b/solution.py
@@ -63,7 +63,7 @@
         aggregated, act_grad, (((0,), (0,)), ((), ())), preferred_element_type=jnp.float32
     )
     node_total = own_rows * lax.axis_size("blk") * lax.axis_size("rep")
-    grad_weight = lax.psum(local_weight, ("blk", "rep")) / math.sqrt(node_total)
+    grad_weight = lax.psum(lax.psum(local_weight, "blk"), "rep") / math.sqrt(node_total)
     back_grad = lax.dot_general(
         act_grad, weight, (((1,), (1,)), ((), ())), preferred_element_type=jnp.float32
     )

time: 519 us -> 1010 us (1.95)
  the two profiles are of different devices: /device:TPU:23 before, /device:TPU:94 now
where the time goes in v1:
time: 1010 us
  waiting for transfers between devices  728 us (72%)
  starting transfers between devices  120 us (12%)
  local copies, waits for them, and re-layouts  65.1 us (6%)
  matrix products  36.1 us (4%)
  other arithmetic  26.3 us (3%)
  blocking collectives  15.5 us (2%)
  between operations  13.9 us (1%)
    psum x1, waiting for transfers between devices, per_device(): lax.psum(local_weight, 'blk')  546 us
    ppermute x30, waiting for transfers between devices, passed_along(): return lax.ppermute(block, axis, route)  137 us
    ppermute x30, starting transfers between devices, passed_along(): return lax.ppermute(block, axis, route)  120 us
    reduce_scatter x1, waiting for transfers between devices, per_device(): lax.psum_scatter(slab_partial, 'rep', scatter_dimension=0, tiled=True)  44.4 us
    dynamic_slice x31, local copies, waits for them, and re-layouts, load_distance(): lax.dynamic_index_in_dim(count_stack, distance, 0, keepdims=False)  28.6 us
    dot_general x16, matrix products, scatter_rows(): jnp.einsum('kij,kif->jf', tile_block, picked, preferred_element_type=jnp....  21.2 us
  transfers between devices with their start and end apart: 33, of which 17 were waited for; matrix products, arithmetic and copies ran while one was open for 11% of the time, Pallas kernels for 0%

profile of v1, /device:TPU:94, one launch (start us, length us, event | category | flops | bytes accessed | tf_op | source)
XLA Modules:
  0.0 1006.7 jit_solution(4041459939695832653)
XLA Ops:
  14.3 153.9 %while.34 = (s32[]{:T(128)}, f32[8,128,256]{2,1,0:T(8,128)S(1)}, bf16[128,256]{1,0:T(8,128)(2,1)S(1)}, s32[16,8]{1,0:T(8,128)S(1)}, s32[16]{0:T(128)}, /*index=5...) while((s32[]{:T(128)}, f32[8,128,256]{2,1,0:T(8,128)S(1)}, ...), condition=%wide.region_2.4_spmd.clone.clone, body=%wide.region_0.3_spmd.clone.clone.sunk | while | flops 68027656 | bytes 3871199 | solution.py:51
  22.3 6.0 collective-permute-start.1
  32.7 6.0 collective-permute-start.1
  43.1 6.0 collective-permute-start.1
  53.5 6.0 collective-permute-start.1
  63.8 6.0 collective-permute-start.1
  74.2 6.0 collective-permute-start.1
  84.6 6.0 collective-permute-start.1
  95.0 6.7 collective-permute-start.1
  116.4 6.0 collective-permute-start.1
  126.7 6.0 collective-permute-start.1
  137.1 6.0 collective-permute-start.1
  147.5 6.0 collective-permute-start.1
  170.3 44.4 %reduce-scatter.2.cloned.1.call-done = f32[128,256]{1,0:T(8,128)} async-done(((f32[1024,256]{1,0:T(8,128)}), f32[128,256]{1,0:T(8,128)}) %reduce-scatter.2.cloned.1.call-update) | async-done | bytes 131088 | tf_op jit(solution)/shard_map/reduce_scatter | solution.py:54
  218.6 15.5 %all_gather.3 = bf16[1024,256]{1,0:T(8,128)(2,1)S(1)} all-gather(bf16[128,256]{1,0:T(8,128)(2,1)S(1)} %fusion.25), channel_id=1, replica_groups=mesh['blk'=64,'rep'=8] {'rep'}, dimensions={0}, use_global_device_ids=true | all-gather | bytes 589824 | tf_op jit(solution)/shard_map/all_gather | solution.py:71
  234.7 545.9 %all-reduce.3.cloned.1.call-done = f32[256,256]{1,0:T(8,128)} async-done(((f32[256,256]{1,0:T(8,128)}), f32[256,256]{1,0:T(8,128)}) %all-reduce.3.cloned.1.call-update) | async-done | bytes 262160 | tf_op jit(solution)/shard_map/psum | solution.py:66
  780.6 216.0 %while.33 = (s32[]{:T(128)}, f32[128,256]{1,0:T(8,128)S(1)}, bf16[16,8,128,128]{3,2,1,0:T(8,128)(2,1)}, s32[16]{0:T(128)S(1)}, s32[16,8]{1,0:T(8,128)S(1)}, /*in...) while((s32[]{:T(128)}, f32[128,256]{1,0:T(8,128)S(1)}, ...), condition=%wide.region_8.11_spmd.clone, body=%wide.region_7.10_spmd.clone.sunk | while | flops 67667008 | bytes 2625907 | solution.py:88
  788.4 6.5 collective-permute-done
  800.0 9.3 collective-permute-done
  814.3 9.3 collective-permute-done
  828.7 9.2 collective-permute-done
  843.0 9.3 collective-permute-done
  857.4 9.1 collective-permute-done
  871.6 9.1 collective-permute-done
  885.8 9.1 collective-permute-done
  900.0 9.4 collective-permute-done
  914.4 10.5 %collective-permute-done = f32[128,256]{1,0:T(8,128)S(1)} collective-permute-done((f32[128,256]{1,0:T(8,128)S(1)}, f32[128,256]{1,0:T(8,128)S(1)}, u32[]{:S(2)}, u32[]{:S(2)}) %collective-permute-start) | collective-permute-done | bytes 131104 | tf_op jit(solution)/shard_map/while/body/eval_jaxpr/ppermute | solution.py:11
  930.0 9.7 collective-permute-done
  944.8 9.1 collective-permute-done
  959.0 9.1 collective-permute-done
  973.2 9.1 collective-permute-done
  987.5 9.1 collective-permute-done
  (294 shorter events, 174.9 us)
Async XLA Ops:
  7.2 207.5 %reduce-scatter.2.cloned.1.call-start = ((), (), s32[]{:S(2)}) async-start(), calls=%async_computation.1 | async-start | bytes 1179648 | tf_op jit(solution)/shard_map/reduce_scatter | solution.py:54
  22.3 10.3 %collective-permute-start.1 = (bf16[128,256]{1,0:T(8,128)(2,1)S(1)}, bf16[128,256]{1,0:T(8,128)(2,1)S(1)}, u32[]{:S(2)}, u32[]{:S(2)}) collective-permute-start(bf16[128,256]{1,0:T(8,128)(2,1)S(1)} %copy.29), channel_id=1, source_target_pairs={{504,0},{0,8},{8,16},{16,24},{24,32},{32,40},{40,48},{48,56},{56,6... | collective-permute-start | bytes 196616 | tf_op jit(solution)/shard_map/while/body/eval_jaxpr/ppermute | solution.py:11
  32.7 10.3 %collective-permute-start.1 = (bf16[128,256]{1,0:T(8,128)(2,1)S(1)}, bf16[128,256]{1,0:T(8,128)(2,1)S(1)}, u32[]{:S(2)}, u32[]{:S(2)}) collective-permute-start(bf16[128,256]{1,0:T(8,128)(2,1)S(1)} %copy.29), channel_id=1, source_target_pairs={{504,0},{0,8},{8,16},{16,24},{24,32},{32,40},{40,48},{48,56},{56,6... | collective-permute-start | bytes 196616 | tf_op jit(solution)/shard_map/while/body/eval_jaxpr/ppermute | solution.py:11
  43.1 10.3 %collective-permute-start.1 = (bf16[128,256]{1,0:T(8,128)(2,1)S(1)}, bf16[128,256]{1,0:T(8,128)(2,1)S(1)}, u32[]{:S(2)}, u32[]{:S(2)}) collective-permute-start(bf16[128,256]{1,0:T(8,128)(2,1)S(1)} %copy.29), channel_id=1, source_target_pairs={{504,0},{0,8},{8,16},{16,24},{24,32},{32,40},{40,48},{48,56},{56,6... | collective-permute-start | bytes 196616 | tf_op jit(solution)/shard_map/while/body/eval_jaxpr/ppermute | solution.py:11
  53.5 10.3 %collective-permute-start.1 = (bf16[128,256]{1,0:T(8,128)(2,1)S(1)}, bf16[128,256]{1,0:T(8,128)(2,1)S(1)}, u32[]{:S(2)}, u32[]{:S(2)}) collective-permute-start(bf16[128,256]{1,0:T(8,128)(2,1)S(1)} %copy.29), channel_id=1, source_target_pairs={{504,0},{0,8},{8,16},{16,24},{24,32},{32,40},{40,48},{48,56},{56,6... | collective-permute-start | bytes 196616 | tf_op jit(solution)/shard_map/while/body/eval_jaxpr/ppermute | solution.py:11
  63.8 10.3 %collective-permute-start.1 = (bf16[128,256]{1,0:T(8,128)(2,1)S(1)}, bf16[128,256]{1,0:T(8,128)(2,1)S(1)}, u32[]{:S(2)}, u32[]{:S(2)}) collective-permute-start(bf16[128,256]{1,0:T(8,128)(2,1)S(1)} %copy.29), channel_id=1, source_target_pairs={{504,0},{0,8},{8,16},{16,24},{24,32},{32,40},{40,48},{48,56},{56,6... | collective-permute-start | bytes 196616 | tf_op jit(solution)/shard_map/while/body/eval_jaxpr/ppermute | solution.py:11
  74.2 10.3 %collective-permute-start.1 = (bf16[128,256]{1,0:T(8,128)(2,1)S(1)}, bf16[128,256]{1,0:T(8,128)(2,1)S(1)}, u32[]{:S(2)}, u32[]{:S(2)}) collective-permute-start(bf16[128,256]{1,0:T(8,128)(2,1)S(1)} %copy.29), channel_id=1, source_target_pairs={{504,0},{0,8},{8,16},{16,24},{24,32},{32,40},{40,48},{48,56},{56,6... | collective-permute-start | bytes 196616 | tf_op jit(solution)/shard_map/while/body/eval_jaxpr/ppermute | solution.py:11
  84.6 10.3 %collective-permute-start.1 = (bf16[128,256]{1,0:T(8,128)(2,1)S(1)}, bf16[128,256]{1,0:T(8,128)(2,1)S(1)}, u32[]{:S(2)}, u32[]{:S(2)}) collective-permute-start(bf16[128,256]{1,0:T(8,128)(2,1)S(1)} %copy.29), channel_id=1, source_target_pairs={{504,0},{0,8},{8,16},{16,24},{24,32},{32,40},{40,48},{48,56},{56,6... | collective-permute-start | bytes 196616 | tf_op jit(solution)/shard_map/while/body/eval_jaxpr/ppermute | solution.py:11
  95.0 11.0 %collective-permute-start.1 = (bf16[128,256]{1,0:T(8,128)(2,1)S(1)}, bf16[128,256]{1,0:T(8,128)(2,1)S(1)}, u32[]{:S(2)}, u32[]{:S(2)}) collective-permute-start(bf16[128,256]{1,0:T(8,128)(2,1)S(1)} %copy.29), channel_id=1, source_target_pairs={{504,0},{0,8},{8,16},{16,24},{24,32},{32,40},{40,48},{48,56},{56,6... | collective-permute-start | bytes 196616 | tf_op jit(solution)/shard_map/while/body/eval_jaxpr/ppermute | solution.py:11
  106.0 10.3 %collective-permute-start.1 = (bf16[128,256]{1,0:T(8,128)(2,1)S(1)}, bf16[128,256]{1,0:T(8,128)(2,1)S(1)}, u32[]{:S(2)}, u32[]{:S(2)}) collective-permute-start(bf16[128,256]{1,0:T(8,128)(2,1)S(1)} %copy.29), channel_id=1, source_target_pairs={{504,0},{0,8},{8,16},{16,24},{24,32},{32,40},{40,48},{48,56},{56,6... | collective-permute-start | bytes 196616 | tf_op jit(solution)/shard_map/while/body/eval_jaxpr/ppermute | solution.py:11
  116.4 10.3 %collective-permute-start.1 = (bf16[128,256]{1,0:T(8,128)(2,1)S(1)}, bf16[128,256]{1,0:T(8,128)(2,1)S(1)}, u32[]{:S(2)}, u32[]{:S(2)}) collective-permute-start(bf16[128,256]{1,0:T(8,128)(2,1)S(1)} %copy.29), channel_id=1, source_target_pairs={{504,0},{0,8},{8,16},{16,24},{24,32},{32,40},{40,48},{48,56},{56,6... | collective-permute-start | bytes 196616 | tf_op jit(solution)/shard_map/while/body/eval_jaxpr/ppermute | solution.py:11
  126.7 10.3 %collective-permute-start.1 = (bf16[128,256]{1,0:T(8,128)(2,1)S(1)}, bf16[128,256]{1,0:T(8,128)(2,1)S(1)}, u32[]{:S(2)}, u32[]{:S(2)}) collective-permute-start(bf16[128,256]{1,0:T(8,128)(2,1)S(1)} %copy.29), channel_id=1, source_target_pairs={{504,0},{0,8},{8,16},{16,24},{24,32},{32,40},{40,48},{48,56},{56,6... | collective-permute-start | bytes 196616 | tf_op jit(solution)/shard_map/while/body/eval_jaxpr/ppermute | solution.py:11
  137.1 10.3 %collective-permute-start.1 = (bf16[128,256]{1,0:T(8,128)(2,1)S(1)}, bf16[128,256]{1,0:T(8,128)(2,1)S(1)}, u32[]{:S(2)}, u32[]{:S(2)}) collective-permute-start(bf16[128,256]{1,0:T(8,128)(2,1)S(1)} %copy.29), channel_id=1, source_target_pairs={{504,0},{0,8},{8,16},{16,24},{24,32},{32,40},{40,48},{48,56},{56,6... | collective-permute-start | bytes 196616 | tf_op jit(solution)/shard_map/while/body/eval_jaxpr/ppermute | solution.py:11
  147.5 10.3 %collective-permute-start.1 = (bf16[128,256]{1,0:T(8,128)(2,1)S(1)}, bf16[128,256]{1,0:T(8,128)(2,1)S(1)}, u32[]{:S(2)}, u32[]{:S(2)}) collective-permute-start(bf16[128,256]{1,0:T(8,128)(2,1)S(1)} %copy.29), channel_id=1, source_target_pairs={{504,0},{0,8},{8,16},{16,24},{24,32},{32,40},{40,48},{48,56},{56,6... | collective-permute-start | bytes 196616 | tf_op jit(solution)/shard_map/while/body/eval_jaxpr/ppermute | solution.py:11
  157.8 10.3 %collective-permute-start.1 = (bf16[128,256]{1,0:T(8,128)(2,1)S(1)}, bf16[128,256]{1,0:T(8,128)(2,1)S(1)}, u32[]{:S(2)}, u32[]{:S(2)}) collective-permute-start(bf16[128,256]{1,0:T(8,128)(2,1)S(1)} %copy.29), channel_id=1, source_target_pairs={{504,0},{0,8},{8,16},{16,24},{24,32},{32,40},{40,48},{48,56},{56,6... | collective-permute-start | bytes 196616 | tf_op jit(solution)/shard_map/while/body/eval_jaxpr/ppermute | solution.py:11
  169.6 611.0 %all-reduce.3.cloned.1.call-start = ((), (), s32[]{:S(2)}) async-start(), calls=%async_computation.2 | async-start | bytes 524288 | tf_op jit(solution)/shard_map/psum | solution.py:66
  218.4 780.1 %all-reduce.5.cloned.1.call-start = ((), (), s32[]{:S(2)}) async-start(), calls=%async_computation.3 | async-start | bytes 524288 | tf_op jit(solution)/shard_map/psum | solution.py:66
  783.8 11.1 %collective-permute-start = (f32[128,256]{1,0:T(8,128)S(1)}, f32[128,256]{1,0:T(8,128)S(1)}, u32[]{:S(2)}, u32[]{:S(2)}) collective-permute-start(f32[128,256]{1,0:T(8,128)S(1)} %fusion.53), channel_id=1, source_target_pairs={{8,0},{16,8},{24,16},{32,24},{40,32},{48,40},{56,48},{64,56},{72,6... | collective-permute-start | bytes 393224 | tf_op jit(solution)/shard_map/while/body/eval_jaxpr/ppermute | solution.py:11
  798.0 11.2 %collective-permute-start = (f32[128,256]{1,0:T(8,128)S(1)}, f32[128,256]{1,0:T(8,128)S(1)}, u32[]{:S(2)}, u32[]{:S(2)}) collective-permute-start(f32[128,256]{1,0:T(8,128)S(1)} %fusion.53), channel_id=1, source_target_pairs={{8,0},{16,8},{24,16},{32,24},{40,32},{48,40},{56,48},{64,56},{72,6... | collective-permute-start | bytes 393224 | tf_op jit(solution)/shard_map/while/body/eval_jaxpr/ppermute | solution.py:11
  812.4 11.3 %collective-permute-start = (f32[128,256]{1,0:T(8,128)S(1)}, f32[128,256]{1,0:T(8,128)S(1)}, u32[]{:S(2)}, u32[]{:S(2)}) collective-permute-start(f32[128,256]{1,0:T(8,128)S(1)} %fusion.53), channel_id=1, source_target_pairs={{8,0},{16,8},{24,16},{32,24},{40,32},{48,40},{56,48},{64,56},{72,6... | collective-permute-start | bytes 393224 | tf_op jit(solution)/shard_map/while/body/eval_jaxpr/ppermute | solution.py:11
  826.8 11.1 %collective-permute-start = (f32[128,256]{1,0:T(8,128)S(1)}, f32[128,256]{1,0:T(8,128)S(1)}, u32[]{:S(2)}, u32[]{:S(2)}) collective-permute-start(f32[128,256]{1,0:T(8,128)S(1)} %fusion.53), channel_id=1, source_target_pairs={{8,0},{16,8},{24,16},{32,24},{40,32},{48,40},{56,48},{64,56},{72,6... | collective-permute-start | bytes 393224 | tf_op jit(solution)/shard_map/while/body/eval_jaxpr/ppermute | solution.py:11
  841.0 11.2 %collective-permute-start = (f32[128,256]{1,0:T(8,128)S(1)}, f32[128,256]{1,0:T(8,128)S(1)}, u32[]{:S(2)}, u32[]{:S(2)}) collective-permute-start(f32[128,256]{1,0:T(8,128)S(1)} %fusion.53), channel_id=1, source_target_pairs={{8,0},{16,8},{24,16},{32,24},{40,32},{48,40},{56,48},{64,56},{72,6... | collective-permute-start | bytes 393224 | tf_op jit(solution)/shard_map/while/body/eval_jaxpr/ppermute | solution.py:11
  855.4 11.1 %collective-permute-start = (f32[128,256]{1,0:T(8,128)S(1)}, f32[128,256]{1,0:T(8,128)S(1)}, u32[]{:S(2)}, u32[]{:S(2)}) collective-permute-start(f32[128,256]{1,0:T(8,128)S(1)} %fusion.53), channel_id=1, source_target_pairs={{8,0},{16,8},{24,16},{32,24},{40,32},{48,40},{56,48},{64,56},{72,6... | collective-permute-start | bytes 393224 | tf_op jit(solution)/shard_map/while/body/eval_jaxpr/ppermute | solution.py:11
  869.6 11.1 %collective-permute-start = (f32[128,256]{1,0:T(8,128)S(1)}, f32[128,256]{1,0:T(8,128)S(1)}, u32[]{:S(2)}, u32[]{:S(2)}) collective-permute-start(f32[128,256]{1,0:T(8,128)S(1)} %fusion.53), channel_id=1, source_target_pairs={{8,0},{16,8},{24,16},{32,24},{40,32},{48,40},{56,48},{64,56},{72,6... | collective-permute-start | bytes 393224 | tf_op jit(solution)/shard_map/while/body/eval_jaxpr/ppermute | solution.py:11
  883.9 11.1 %collective-permute-start = (f32[128,256]{1,0:T(8,128)S(1)}, f32[128,256]{1,0:T(8,128)S(1)}, u32[]{:S(2)}, u32[]{:S(2)}) collective-permute-start(f32[128,256]{1,0:T(8,128)S(1)} %fusion.53), channel_id=1, source_target_pairs={{8,0},{16,8},{24,16},{32,24},{40,32},{48,40},{56,48},{64,56},{72,6... | collective-permute-start | bytes 393224 | tf_op jit(solution)/shard_map/while/body/eval_jaxpr/ppermute | solution.py:11
  898.1 11.3 %collective-permute-start = (f32[128,256]{1,0:T(8,128)S(1)}, f32[128,256]{1,0:T(8,128)S(1)}, u32[]{:S(2)}, u32[]{:S(2)}) collective-permute-start(f32[128,256]{1,0:T(8,128)S(1)} %fusion.53), channel_id=1, source_target_pairs={{8,0},{16,8},{24,16},{32,24},{40,32},{48,40},{56,48},{64,56},{72,6... | collective-permute-start | bytes 393224 | tf_op jit(solution)/shard_map/while/body/eval_jaxpr/ppermute | solution.py:11
  912.5 12.4 %collective-permute-start = (f32[128,256]{1,0:T(8,128)S(1)}, f32[128,256]{1,0:T(8,128)S(1)}, u32[]{:S(2)}, u32[]{:S(2)}) collective-permute-start(f32[128,256]{1,0:T(8,128)S(1)} %fusion.53), channel_id=1, source_target_pairs={{8,0},{16,8},{24,16},{32,24},{40,32},{48,40},{56,48},{64,56},{72,6... | collective-permute-start | bytes 393224 | tf_op jit(solution)/shard_map/while/body/eval_jaxpr/ppermute | solution.py:11
  928.1 11.6 %collective-permute-start = (f32[128,256]{1,0:T(8,128)S(1)}, f32[128,256]{1,0:T(8,128)S(1)}, u32[]{:S(2)}, u32[]{:S(2)}) collective-permute-start(f32[128,256]{1,0:T(8,128)S(1)} %fusion.53), channel_id=1, source_target_pairs={{8,0},{16,8},{24,16},{32,24},{40,32},{48,40},{56,48},{64,56},{72,6... | collective-permute-start | bytes 393224 | tf_op jit(solution)/shard_map/while/body/eval_jaxpr/ppermute | solution.py:11
  942.9 11.1 %collective-permute-start = (f32[128,256]{1,0:T(8,128)S(1)}, f32[128,256]{1,0:T(8,128)S(1)}, u32[]{:S(2)}, u32[]{:S(2)}) collective-permute-start(f32[128,256]{1,0:T(8,128)S(1)} %fusion.53), channel_id=1, source_target_pairs={{8,0},{16,8},{24,16},{32,24},{40,32},{48,40},{56,48},{64,56},{72,6... | collective-permute-start | bytes 393224 | tf_op jit(solution)/shard_map/while/body/eval_jaxpr/ppermute | solution.py:11
  957.1 11.1 %collective-permute-start = (f32[128,256]{1,0:T(8,128)S(1)}, f32[128,256]{1,0:T(8,128)S(1)}, u32[]{:S(2)}, u32[]{:S(2)}) collective-permute-start(f32[128,256]{1,0:T(8,128)S(1)} %fusion.53), channel_id=1, source_target_pairs={{8,0},{16,8},{24,16},{32,24},{40,32},{48,40},{56,48},{64,56},{72,6... | collective-permute-start | bytes 393224 | tf_op jit(solution)/shard_map/while/body/eval_jaxpr/ppermute | solution.py:11
  971.3 11.1 %collective-permute-start = (f32[128,256]{1,0:T(8,128)S(1)}, f32[128,256]{1,0:T(8,128)S(1)}, u32[]{:S(2)}, u32[]{:S(2)}) collective-permute-start(f32[128,256]{1,0:T(8,128)S(1)} %fusion.53), channel_id=1, source_target_pairs={{8,0},{16,8},{24,16},{32,24},{40,32},{48,40},{56,48},{64,56},{72,6... | collective-permute-start | bytes 393224 | tf_op jit(solution)/shard_map/while/body/eval_jaxpr/ppermute | solution.py:11
  985.5 11.1 %collective-permute-start = (f32[128,256]{1,0:T(8,128)S(1)}, f32[128,256]{1,0:T(8,128)S(1)}, u32[]{:S(2)}, u32[]{:S(2)}) collective-permute-start(f32[128,256]{1,0:T(8,128)S(1)} %fusion.53), channel_id=1, source_target_pairs={{8,0},{16,8},{24,16},{32,24},{40,32},{48,40},{56,48},{64,56},{72,6... | collective-permute-start | bytes 393224 | tf_op jit(solution)/shard_map/while/body/eval_jaxpr/ppermute | solution.py:11
  (4 other events, 1028.3 us)
Sparse Core Ops, SparseCore 0:
  169.7 44.9 reduce-scatter.1
  218.5 562.0 all-reduce.2
  783.5 79.3 all-reduce.4
